TPU v7x, 32 devices: a whole 2x2x4 slice. The times are simulated.
32 devices in a mesh: plant: 8 (over z, core), col: 4 (over y, x).
Axes of the slice: x: 2, y: 2, z: 4, core: 2. Of those that a mesh axis runs over, the one named last changes fastest.
Arguments:
- tiles: bfloat16 [8, 4, 48, 256, 256], P('plant', 'col'), may hold values from -0.109375 to 0.109375
- tile_row: int32 [8, 4, 48], P('plant', 'col'), may hold values from 0 to 15
- tile_col: int32 [8, 4, 48], P('plant', 'col'), may hold values from 0 to 63
- row_count: int32 [8], P('plant'), may hold values from 2048 to 4096, as said below
- x_start: float32 [32, 65536], P(None, 'col'), may hold values from 0 to 1
- y_start: float32 [32, 32768], P(None, 'plant'), may hold values from 0 to 1
- cost: float32 [65536], P('col'), may hold values from -3 to 3
- upper: float32 [65536], P('col'), may hold values from 0.5 to 2
- demand: float32 [32, 32768], P(None, 'plant'), may hold values from -6 to 6
- tau: float32 [32], replicated, may hold values from 0.2 to 1
- sigma: float32 [32], replicated, may hold values from 0.2 to 1
Outputs:
- primal: float32 [32, 65536], P(None, 'col')
- dual: float32 [32, 32768], P(None, 'plant')
Inputs may be any that keep to these rules, and one draw needn't show every extreme that they name: Each plant block has row_count live rows, the first ones of its block; at least one plant block is full. `tile_row`: tiles at the same position add up.
All inputs are finite; a program needn't handle non-finite values.
Results may differ from a plain program's by a relative error of at most 0.003.
Values sent between devices are 32-bit elements; how exact they have to be, the bound alone decides.
No kernel may reach another device: no remote copies, remote signals or barrier semaphores. Data moves between devices by JAX's collectives and lax.ppermute only.
A program may use at most 64 MiB of HBM per device.

v0:
```python
import jax
import jax.numpy as jnp
from jax import lax
from jax.sharding import PartitionSpec as P

ITERS = 3


def body(tiles, tile_row, tile_col, row_count, x_start, y_start, cost, upper, demand, tau, sigma):
    blocks = tiles[0, 0]
    rows = tile_row[0, 0]
    cols = tile_col[0, 0]
    tile_width = blocks.shape[1]
    scenarios, rows_dev = y_start.shape
    col_width = x_start.shape[1]
    row_tiles = rows_dev // tile_width
    col_tiles = col_width // tile_width
    live = (jnp.arange(rows_dev, dtype=jnp.int32) < row_count[0]).astype(jnp.float32)[None, :]
    row_hot = (jnp.arange(row_tiles, dtype=jnp.int32)[:, None] == rows[None, :]).astype(jnp.float32)
    col_hot = (jnp.arange(col_tiles, dtype=jnp.int32)[:, None] == cols[None, :]).astype(jnp.float32)
    step_primal = tau[:, None]
    step_dual = sigma[:, None]
    cost_row = cost[None, :]
    upper_row = upper[None, :]
    primal = x_start
    dual = y_start * live
    for iteration in range(ITERS):
        dual_low = dual.astype(jnp.bfloat16).reshape(scenarios, row_tiles, tile_width)
        picked = jnp.take(dual_low, rows, axis=1)
        contrib = jnp.einsum("str,trc->stc", picked, blocks, preferred_element_type=jnp.float32)
        kty_part = jnp.einsum(
            "kt,stc->skc", col_hot, contrib, precision=lax.Precision.HIGHEST
        ).reshape(scenarios, col_width)
        kty = lax.psum(kty_part, "plant")
        primal_new = jnp.minimum(
            jnp.maximum(primal - step_primal * (cost_row - kty), 0.0), upper_row
        )
        extra = (
            (2.0 * primal_new - primal)
            .astype(jnp.bfloat16)
            .reshape(scenarios, col_tiles, tile_width)
        )
        chosen = jnp.take(extra, cols, axis=1)
        product = jnp.einsum("stc,trc->str", chosen, blocks, preferred_element_type=jnp.float32)
        kx_part = jnp.einsum(
            "kt,str->skr", row_hot, product, precision=lax.Precision.HIGHEST
        ).reshape(scenarios, rows_dev)
        kx = lax.psum(kx_part, "col")
        dual = jnp.maximum(dual + step_dual * (demand - kx), 0.0) * live
        primal = primal_new
    return (primal, dual)


def solution(mesh):
    placed = (
        P("plant", "col", None, None, None),
        P("plant", "col", None),
        P("plant", "col", None),
        P("plant"),
        P(None, "col"),
        P(None, "plant"),
        P("col"),
        P("col"),
        P(None, "plant"),
        P(),
        P(),
    )
    return jax.shard_map(
        body,
        mesh=mesh,
        in_specs=placed,
        out_specs=(P(None, "col"), P(None, "plant")),
        check_vma=False,
    )
```

profile of v0, /device:TPU:0, one launch (start us, length us, event | category | flops | bytes accessed | tf_op | source)
XLA Modules:
  0.0 428.5 jit_solution(13103330824339237959)
XLA Ops:
  11.0 4.0 fusion.24
  15.0 2.1 fusion.22
  17.1 2.5 copy.31
  19.8 67.6 %all-reduce.7.cloned.1.call-done = f32[32,16384]{1,0:T(8,128)} async-done(((f32[32,16384]{1,0:T(8,128)}), f32[32,16384]{1,0:T(8,128)}) %all-reduce.7.cloned.1.call-update) | async-done | bytes 2097168 | tf_op jit(solution)/shard_map/psum | solution.py:34
  87.4 2.2 subtract_convert_fusion.2
  90.7 1.8 gather_fusion.1
  92.6 4.7 %fusion.27 = f32[32,48,256]{2,0,1:T(8,128)S(1)} fusion(bf16[1,1,48,256,256]{4,3,2,1,0:T(8,128)(2,1)} %param.15, bf16[48,32,256]{2,1,0:T(8,128)(2,1)S(1)} %gather_fusion.1, pred[48]{0:T(512)(128)(4,1)S(1)} %compare_and_fusion), kind=kOutput, calls=%fused_computation.37 | convolution fusion | flops 201719808 | bytes 8650800 | tf_op jit(solution)/shard_map/stc,trc->str/dot_general | solution.py:44
  97.4 1.5 fusion.20
  100.2 44.9 %all-reduce.9.cloned.1.call-done = f32[32,4096]{1,0:T(8,128)} async-done(((f32[32,4096]{1,0:T(8,128)}), f32[32,4096]{1,0:T(8,128)}) %all-reduce.9.cloned.1.call-update) | async-done | bytes 524304 | tf_op jit(solution)/shard_map/psum | solution.py:48
  145.2 1.2 fusion.88
  146.4 1.7 gather_fusion.2
  148.1 4.3 fusion.30
  152.4 2.2 fusion.18
  154.5 2.5 copy.33
  157.1 65.0 %all-reduce.11.cloned.1.call-done = f32[32,16384]{1,0:T(8,128)} async-done(((f32[32,16384]{1,0:T(8,128)}), f32[32,16384]{1,0:T(8,128)}) %all-reduce.11.cloned.1.call-update) | async-done | bytes 2097168 | tf_op jit(solution)/shard_map/psum | solution.py:34
  222.1 3.1 subtract_convert_fusion.1
  226.4 2.9 gather_fusion.3
  229.3 5.0 %fusion.33 = f32[32,48,256]{2,0,1:T(8,128)S(1)} fusion(bf16[1,1,48,256,256]{4,3,2,1,0:T(8,128)(2,1)} %param.15, bf16[48,32,256]{2,1,0:T(8,128)(2,1)} %gather_fusion.3, pred[48]{0:T(512)(128)(4,1)S(1)} %copy-done.12), kind=kOutput, calls=%fused_computation.39 | convolution fusion | flops 201719808 | bytes 8650800 | tf_op jit(solution)/shard_map/stc,trc->str/dot_general | solution.py:44
  234.3 1.5 fusion.16
  237.2 44.9 %all-reduce.13.cloned.1.call-done = f32[32,4096]{1,0:T(8,128)} async-done(((f32[32,4096]{1,0:T(8,128)}), f32[32,4096]{1,0:T(8,128)}) %all-reduce.13.cloned.1.call-update) | async-done | bytes 524304 | tf_op jit(solution)/shard_map/psum | solution.py:48
  282.1 1.5 fusion.87
  283.6 1.7 gather_fusion.4
  285.2 4.3 fusion.36
  289.5 2.1 fusion.14
  291.6 2.5 copy.35
  294.3 65.0 %all-reduce.15.cloned.1.call-done = f32[32,16384]{1,0:T(8,128)} async-done(((f32[32,16384]{1,0:T(8,128)}), f32[32,16384]{1,0:T(8,128)}) %all-reduce.15.cloned.1.call-update) | async-done | bytes 2097168 | tf_op jit(solution)/shard_map/psum | solution.py:34
  359.3 5.4 %subtract_convert_fusion = (bf16[32,16384]{1,0:T(8,128)(2,1)S(1)}, f32[32,16384]{1,0:T(8,128)}) fusion(f32[32,16384]{1,0:T(8,128)} %all-reduce.11.cloned.1.call-done, f32[16384]{0:T(1024)S(1)} %copy-done.4, f32[32,16384]{1,0:T(8,128)S(1)} %copy-done, f32[32,16384]{1,0:T(8,128)} %all-reduce.7.cloned.1.call-done, f32[16384]{0:T(1024)S(1)} %copy-done.5, ...), kind=kLoop, calls=%fused_computation.18 | loop fusion | flops 9437184 | bytes 11665536 | tf_op jit(solution)/shard_map/convert_element_type | solution.py:40
  364.8 1.7 gather_fusion.5
  366.5 5.0 %fusion.39 = f32[32,48,256]{2,0,1:T(8,128)S(1)} fusion(bf16[1,1,48,256,256]{4,3,2,1,0:T(8,128)(2,1)} %param.15, bf16[48,32,256]{2,1,0:T(8,128)(2,1)} %gather_fusion.5, pred[48]{0:T(512)(128)(4,1)S(1)} %copy-done.13), kind=kOutput, calls=%fused_computation.41 | convolution fusion | flops 201719808 | bytes 8650800 | tf_op jit(solution)/shard_map/stc,trc->str/dot_general | solution.py:44
  371.5 1.5 fusion.12
  374.2 45.1 %all-reduce.17.cloned.1.call-done = f32[32,4096]{1,0:T(8,128)} async-done(((f32[32,4096]{1,0:T(8,128)}), f32[32,4096]{1,0:T(8,128)}) %all-reduce.17.cloned.1.call-update) | async-done | bytes 524304 | tf_op jit(solution)/shard_map/psum | solution.py:48
  419.3 2.3 maximum_multiply_fusion
  (78 shorter events, 9.6 us)
Async XLA Ops:
  7.2 80.3 %all-reduce.7.cloned.1.call-start = ((), (), s32[]{:S(2)}) async-start(), calls=%async_computation | async-start | bytes 4194304 | tf_op jit(solution)/shard_map/psum | solution.py:34
  7.9 7.1 %copy-start.14 = (pred[48]{0:T(512)(128)(4,1)}, pred[48]{0:T(512)(128)(4,1)S(1)}, u32[]{:S(2)}) copy-start(pred[48]{0:T(512)(128)(4,1)S(1)} %compare_and_fusion.1) | copy-start | bytes 148
  9.2 5.8 %copy-start.7 = (s32[1024]{0:T(1024)}, s32[1024]{0:T(1024)S(1)}, u32[]{:S(2)}) copy-start(s32[1024]{0:T(1024)S(1)} %pad_clamp_fusion.1) | copy-start | bytes 12292
  11.0 4.0 copy-start.21
  17.1 70.3 %copy-start.4 = (f32[16384]{0:T(1024)S(1)}, f32[16384]{0:T(1024)}, u32[]{:S(2)}) copy-start(f32[16384]{0:T(1024)} %param.22) | copy-start | bytes 196612
  17.1 70.3 %copy-start.5 = (f32[16384]{0:T(1024)S(1)}, f32[16384]{0:T(1024)}, u32[]{:S(2)}) copy-start(f32[16384]{0:T(1024)} %param.21) | copy-start | bytes 196612
  19.7 67.8 %copy-start = (f32[32,16384]{1,0:T(8,128)S(1)}, f32[32,16384]{1,0:T(8,128)}, u32[]{:S(2)}) copy-start(f32[32,16384]{1,0:T(8,128)} %param.19) | copy-start | bytes 6291460
  19.7 67.8 %copy-start.18 = (f32[32]{0:T(128)S(1)}, f32[32]{0:T(128)}, u32[]{:S(2)}) copy-start(f32[32]{0:T(128)} %param.24) | copy-start | bytes 388
  19.7 125.4 %all-reduce.9.cloned.1.call-start = ((), (), s32[]{:S(2)}) async-start(), calls=%async_computation.1 | async-start | bytes 1048576 | tf_op jit(solution)/shard_map/psum | solution.py:48
  19.8 70.9 %copy-start.6 = (s32[1024]{0:T(1024)}, s32[1024]{0:T(1024)S(1)}, u32[]{:S(2)}) copy-start(s32[1024]{0:T(1024)S(1)} %pad_clamp_fusion) | copy-start | bytes 12292
  19.8 72.8 %copy-start.11 = (pred[48]{0:T(512)(128)(4,1)}, pred[48]{0:T(512)(128)(4,1)S(1)}, u32[]{:S(2)}) copy-start(pred[48]{0:T(512)(128)(4,1)S(1)} %compare_and_fusion) | copy-start | bytes 148
  92.6 4.8 %copy-start.8 = (s32[1,1,48]{2,1,0:T(1,128)S(1)}, s32[1,1,48]{2,1,0:T(1,128)}, u32[]{:S(2)}) copy-start(s32[1,1,48]{2,1,0:T(1,128)} %param.16) | copy-start | bytes 580
  97.3 47.8 %copy-start.1 = (f32[32,4096]{1,0:T(8,128)S(1)}, f32[32,4096]{1,0:T(8,128)}, u32[]{:S(2)}) copy-start(f32[32,4096]{1,0:T(8,128)} %param.20) | copy-start | bytes 1572868
  97.3 47.8 %copy-start.2 = (f32[32,4096]{1,0:T(8,128)S(1)}, f32[32,4096]{1,0:T(8,128)}, u32[]{:S(2)}) copy-start(f32[32,4096]{1,0:T(8,128)} %param.23) | copy-start | bytes 1572868
  97.3 47.8 %copy-start.15 = (f32[32]{0:T(128)S(1)}, f32[32]{0:T(128)}, u32[]{:S(2)}) copy-start(f32[32]{0:T(128)} %param.25) | copy-start | bytes 388
  100.0 122.1 %all-reduce.11.cloned.1.call-start = ((), (), s32[]{:S(2)}) async-start(), calls=%async_computation.2 | async-start | bytes 4194304 | tf_op jit(solution)/shard_map/psum | solution.py:34
  148.1 4.3 copy-start.22
  157.0 65.1 %copy-start.19 = (f32[32]{0:T(128)S(1)}, f32[32]{0:T(128)}, u32[]{:S(2)}) copy-start(f32[32]{0:T(128)} %param.24) | copy-start | bytes 388
  157.1 125.0 %all-reduce.13.cloned.1.call-start = ((), (), s32[]{:S(2)}) async-start(), calls=%async_computation.3 | async-start | bytes 1048576 | tf_op jit(solution)/shard_map/psum | solution.py:48
  225.3 4.0 copy-start.12
  229.3 5.0 %copy-start.9 = (s32[1,1,48]{2,1,0:T(1,128)S(1)}, s32[1,1,48]{2,1,0:T(1,128)}, u32[]{:S(2)}) copy-start(s32[1,1,48]{2,1,0:T(1,128)} %param.16) | copy-start | bytes 580
  234.3 47.8 %copy-start.16 = (f32[32]{0:T(128)S(1)}, f32[32]{0:T(128)}, u32[]{:S(2)}) copy-start(f32[32]{0:T(128)} %param.25) | copy-start | bytes 388
  236.9 122.3 %all-reduce.15.cloned.1.call-start = ((), (), s32[]{:S(2)}) async-start(), calls=%async_computation.4 | async-start | bytes 4194304 | tf_op jit(solution)/shard_map/psum | solution.py:34
  285.2 4.3 copy-start.23
  294.2 65.1 %copy-start.20 = (f32[32]{0:T(128)S(1)}, f32[32]{0:T(128)}, u32[]{:S(2)}) copy-start(f32[32]{0:T(128)} %param.24) | copy-start | bytes 388
  294.2 125.1 %all-reduce.17.cloned.1.call-start = ((), (), s32[]{:S(2)}) async-start(), calls=%async_computation.5 | async-start | bytes 1048576 | tf_op jit(solution)/shard_map/psum | solution.py:48
  364.7 1.8 copy-start.13
  366.5 5.0 %copy-start.10 = (s32[1,1,48]{2,1,0:T(1,128)S(1)}, s32[1,1,48]{2,1,0:T(1,128)}, u32[]{:S(2)}) copy-start(s32[1,1,48]{2,1,0:T(1,128)} %param.16) | copy-start | bytes 580
  371.5 47.8 %copy-start.3 = (f32[32,4096]{1,0:T(8,128)S(1)}, f32[32,4096]{1,0:T(8,128)}, u32[]{:S(2)}) copy-start(f32[32,4096]{1,0:T(8,128)} %all-reduce.9.cloned.1.call-done) | copy-start | bytes 1572868
  371.5 47.8 %copy-start.17 = (f32[32]{0:T(128)S(1)}, f32[32]{0:T(128)}, u32[]{:S(2)}) copy-start(f32[32]{0:T(128)} %param.25) | copy-start | bytes 388
Sparse Core Ops, SparseCore 0:
  19.8 67.5 all-reduce.6
  100.1 44.9 all-reduce.8
  157.2 64.8 all-reduce.10
  237.1 44.9 all-reduce.12
  294.3 64.8 all-reduce.14
  374.3 44.9 all-reduce.16
where the time goes:
time: 429 us; the launch traced here: 428 us
  waiting for transfers between devices  333 us (78%)
  matrix products  38.2 us (9%)
  local copies, waits for them, and re-layouts  23.7 us (6%)
  other arithmetic  18.2 us (4%)
  between operations  15.1 us (4%)
    psum x3, waiting for transfers between devices, body(): kty = lax.psum(kty_part, 'plant')  198 us
    psum x3, waiting for transfers between devices, body(): kx = lax.psum(kx_part, 'col')  135 us
    dot_general x3, matrix products, body(): jnp.einsum('stc,trc->str', chosen, blocks, preferred_element_type=jnp.flo...  14.7 us
    dot_general x3, matrix products, body(): jnp.einsum('str,trc->stc', picked, blocks, preferred_element_type=jnp.flo...  12.5 us
    unnamed x54, local copies, waits for them, and re-layouts  11 us
    convert_element_type x3, other arithmetic, body(): extra = (2.0 * primal_new - primal).astype(jnp.bfloat16).reshape(scenario...  10.7 us
  transfers between devices with their start and end apart: 6, of which 6 were waited for; matrix products, arithmetic and copies ran while one was open for 0% of the time, Pallas kernels for 0%

commit v1 on v0

--- a/solution.py
+++ b/solution.py
@@ -45,7 +45,7 @@
         kx_part = jnp.einsum(
             "kt,str->skr", row_hot, product, precision=lax.Precision.HIGHEST
         ).reshape(scenarios, rows_dev)
-        kx = lax.psum(kx_part, "col")
+        kx = jnp.sum(lax.all_gather(kx_part, "col"), axis=0)
         dual = jnp.maximum(dual + step_dual * (demand - kx), 0.0) * live
         primal = primal_new
     return (primal, dual)

time: 429 us -> 405 us (0.944)
  waiting for transfers between devices: 333 us -> 303 us
  other arithmetic: 18.2 us -> 23 us
    psum x3 -> x0, waiting for transfers between devices: 135 us -> none  [body(): kx = lax.psum(kx_part, 'col')]
    all_gather x0 -> x3, waiting for transfers between devices: none -> 105 us  [body(): kx = jnp.sum(lax.all_gather(kx_part, 'col'), axis=0)]
    reduce_sum x0 -> x3, other arithmetic: none -> 6.06 us  [body(): kx = jnp.sum(lax.all_gather(kx_part, 'col'), axis=0)]
    unnamed x54 -> x51, local copies, waits for them, and re-layouts: 11 us -> 7.72 us
where the time goes in v1:
time: 405 us; the launch traced here: 404 us
  waiting for transfers between devices  303 us (75%)
  matrix products  38.9 us (10%)
  local copies, waits for them, and re-layouts  24.1 us (6%)
  other arithmetic  23 us (6%)
  between operations  15.2 us (4%)
    psum x3, waiting for transfers between devices, body(): kty = lax.psum(kty_part, 'plant')  198 us
    all_gather x3, waiting for transfers between devices, body(): kx = jnp.sum(lax.all_gather(kx_part, 'col'), axis=0)  105 us
    dot_general x3, matrix products, body(): jnp.einsum('stc,trc->str', chosen, blocks, preferred_element_type=jnp.flo...  14.7 us
    dot_general x3, matrix products, body(): jnp.einsum('str,trc->stc', picked, blocks, preferred_element_type=jnp.flo...  12.5 us
    convert_element_type x3, other arithmetic, body(): extra = (2.0 * primal_new - primal).astype(jnp.bfloat16).reshape(scenario...  10.7 us
  transfers between devices with their start and end apart: 6, of which 6 were waited for; matrix products, arithmetic and copies ran while one was open for 0% of the time, Pallas kernels for 0%

profile of v1, /device:TPU:0, one launch (start us, length us, event | category | flops | bytes accessed | tf_op | source)
XLA Modules:
  0.0 404.5 jit_solution(8562749732752084734)
XLA Ops:
  11.0 4.0 fusion.24
  15.0 2.1 fusion.22
  17.1 2.5 copy.43
  19.8 67.6 %all-reduce.4.cloned.1.call-done = f32[32,16384]{1,0:T(8,128)} async-done(((f32[32,16384]{1,0:T(8,128)}), f32[32,16384]{1,0:T(8,128)}) %all-reduce.4.cloned.1.call-update) | async-done | bytes 2097168 | tf_op jit(solution)/shard_map/psum | solution.py:34
  87.4 2.2 subtract_convert_fusion.2
  90.7 1.8 gather_fusion.1
  92.6 4.7 %fusion.27 = f32[32,48,256]{2,0,1:T(8,128)S(1)} fusion(bf16[1,1,48,256,256]{4,3,2,1,0:T(8,128)(2,1)} %param.15, bf16[48,32,256]{2,1,0:T(8,128)(2,1)S(1)} %gather_fusion.1, pred[48]{0:T(512)(128)(4,1)S(1)} %compare_and_fusion), kind=kOutput, calls=%fused_computation.37 | convolution fusion | flops 201719808 | bytes 8650800 | tf_op jit(solution)/shard_map/stc,trc->str/dot_general | solution.py:44
  97.3 1.5 fusion.42
  100.0 34.9 %all-gather.4.cloned.1.call-done = f32[4,32,4096]{2,1,0:T(8,128)} async-done(((f32[1,32,4096]{2,1,0:T(8,128)}), f32[4,32,4096]{2,1,0:T(8,128)}) %all-gather.4.cloned.1.call-update) | async-done | bytes 2097168 | tf_op jit(solution)/shard_map/all_gather | solution.py:48
  134.9 1.8 reduce_sum.27
  137.9 1.7 gather_fusion.2
  139.6 4.3 %fusion.30 = f32[32,48,256]{2,0,1:T(8,128)S(1)} fusion(bf16[1,1,48,256,256]{4,3,2,1,0:T(8,128)(2,1)} %param.15, bf16[48,32,256]{2,1,0:T(8,128)(2,1)} %gather_fusion.2, pred[48]{0:T(512)(128)(4,1)} %copy-done.14), kind=kOutput, calls=%fused_computation.38 | convolution fusion | flops 201719808 | bytes 8650800 | tf_op jit(solution)/shard_map/str,trc->stc/dot_general | solution.py:30
  143.9 2.1 fusion.18
  146.0 2.5 copy.44
  148.6 65.0 %all-reduce.6.cloned.1.call-done = f32[32,16384]{1,0:T(8,128)} async-done(((f32[32,16384]{1,0:T(8,128)}), f32[32,16384]{1,0:T(8,128)}) %all-reduce.6.cloned.1.call-update) | async-done | bytes 2097168 | tf_op jit(solution)/shard_map/psum | solution.py:34
  213.6 3.1 subtract_convert_fusion.1
  217.9 2.9 gather_fusion.3
  220.7 5.0 %fusion.33 = f32[32,48,256]{2,0,1:T(8,128)S(1)} fusion(bf16[1,1,48,256,256]{4,3,2,1,0:T(8,128)(2,1)} %param.15, bf16[48,32,256]{2,1,0:T(8,128)(2,1)} %gather_fusion.3, pred[48]{0:T(512)(128)(4,1)S(1)} %copy-done.12), kind=kOutput, calls=%fused_computation.39 | convolution fusion | flops 201719808 | bytes 8650800 | tf_op jit(solution)/shard_map/stc,trc->str/dot_general | solution.py:44
  225.7 2.3 fusion.45
  228.1 1.9 all_gather_reshape.10
  230.3 34.8 %all-gather.6.cloned.1.call-done = f32[4,32,4096]{2,1,0:T(8,128)} async-done(((f32[1,32,4096]{2,1,0:T(8,128)}), f32[4,32,4096]{2,1,0:T(8,128)}) %all-gather.6.cloned.1.call-update) | async-done | bytes 2097168 | tf_op jit(solution)/shard_map/all_gather | solution.py:48
  265.1 2.5 reduce_sum.28
  269.2 1.7 gather_fusion.4
  270.8 4.3 %fusion.36 = f32[32,48,256]{2,0,1:T(8,128)S(1)} fusion(bf16[1,1,48,256,256]{4,3,2,1,0:T(8,128)(2,1)} %param.15, bf16[48,32,256]{2,1,0:T(8,128)(2,1)} %gather_fusion.4, pred[48]{0:T(512)(128)(4,1)} %copy-done.14), kind=kOutput, calls=%fused_computation.40 | convolution fusion | flops 201719808 | bytes 8650800 | tf_op jit(solution)/shard_map/str,trc->stc/dot_general | solution.py:30
  275.1 2.1 fusion.14
  277.2 2.5 copy.45
  279.9 65.0 %all-reduce.8.cloned.1.call-done = f32[32,16384]{1,0:T(8,128)} async-done(((f32[32,16384]{1,0:T(8,128)}), f32[32,16384]{1,0:T(8,128)}) %all-reduce.8.cloned.1.call-update) | async-done | bytes 2097168 | tf_op jit(solution)/shard_map/psum | solution.py:34
  344.9 5.4 %subtract_convert_fusion = (bf16[32,16384]{1,0:T(8,128)(2,1)S(1)}, f32[32,16384]{1,0:T(8,128)}) fusion(f32[32,16384]{1,0:T(8,128)} %all-reduce.6.cloned.1.call-done, f32[16384]{0:T(1024)S(1)} %copy-done.4, f32[32,16384]{1,0:T(8,128)S(1)} %copy-done, f32[32,16384]{1,0:T(8,128)} %all-reduce.4.cloned.1.call-done, f32[16384]{0:T(1024)S(1)} %copy-done.5, ...), kind=kLoop, calls=%fused_computation.18 | loop fusion | flops 9437184 | bytes 11665536 | tf_op jit(solution)/shard_map/convert_element_type | solution.py:40
  350.5 1.7 gather_fusion.5
  352.1 5.0 %fusion.39 = f32[32,48,256]{2,0,1:T(8,128)S(1)} fusion(bf16[1,1,48,256,256]{4,3,2,1,0:T(8,128)(2,1)} %param.15, bf16[48,32,256]{2,1,0:T(8,128)(2,1)} %gather_fusion.5, pred[48]{0:T(512)(128)(4,1)S(1)} %copy-done.13), kind=kOutput, calls=%fused_computation.41 | convolution fusion | flops 201719808 | bytes 8650800 | tf_op jit(solution)/shard_map/stc,trc->str/dot_general | solution.py:44
  359.6 35.1 %all-gather.8.cloned.1.call-done = f32[4,32,4096]{2,1,0:T(8,128)} async-done(((f32[1,32,4096]{2,1,0:T(8,128)}), f32[4,32,4096]{2,1,0:T(8,128)}) %all-gather.8.cloned.1.call-update) | async-done | bytes 2097168 | tf_op jit(solution)/shard_map/all_gather | solution.py:48
  394.7 1.8 reduce_sum.29
  (81 shorter events, 13.4 us)
Async XLA Ops:
  7.2 80.3 %all-reduce.4.cloned.1.call-start = ((), (), s32[]{:S(2)}) async-start(), calls=%async_computation | async-start | bytes 4194304 | tf_op jit(solution)/shard_map/psum | solution.py:34
  7.9 7.1 %copy-start.14 = (pred[48]{0:T(512)(128)(4,1)}, pred[48]{0:T(512)(128)(4,1)S(1)}, u32[]{:S(2)}) copy-start(pred[48]{0:T(512)(128)(4,1)S(1)} %compare_and_fusion.1) | copy-start | bytes 148
  9.2 5.8 %copy-start.7 = (s32[1024]{0:T(1024)}, s32[1024]{0:T(1024)S(1)}, u32[]{:S(2)}) copy-start(s32[1024]{0:T(1024)S(1)} %pad_clamp_fusion.1) | copy-start | bytes 12292
  11.0 4.0 copy-start.21
  17.1 70.3 %copy-start.4 = (f32[16384]{0:T(1024)S(1)}, f32[16384]{0:T(1024)}, u32[]{:S(2)}) copy-start(f32[16384]{0:T(1024)} %param.22) | copy-start | bytes 196612
  17.1 70.3 %copy-start.5 = (f32[16384]{0:T(1024)S(1)}, f32[16384]{0:T(1024)}, u32[]{:S(2)}) copy-start(f32[16384]{0:T(1024)} %param.21) | copy-start | bytes 196612
  19.7 67.8 %copy-start = (f32[32,16384]{1,0:T(8,128)S(1)}, f32[32,16384]{1,0:T(8,128)}, u32[]{:S(2)}) copy-start(f32[32,16384]{1,0:T(8,128)} %param.19) | copy-start | bytes 6291460
  19.7 67.8 %copy-start.18 = (f32[32]{0:T(128)S(1)}, f32[32]{0:T(128)}, u32[]{:S(2)}) copy-start(f32[32]{0:T(128)} %param.24) | copy-start | bytes 388
  19.7 115.2 %all-gather.4.cloned.1.call-start = ((), (), s32[]{:S(2)}) async-start(), calls=%async_computation.1 | async-start | bytes 2621440 | tf_op jit(solution)/shard_map/all_gather | solution.py:48
  19.8 70.9 %copy-start.6 = (s32[1024]{0:T(1024)}, s32[1024]{0:T(1024)S(1)}, u32[]{:S(2)}) copy-start(s32[1024]{0:T(1024)S(1)} %pad_clamp_fusion) | copy-start | bytes 12292
  19.8 72.8 %copy-start.11 = (pred[48]{0:T(512)(128)(4,1)}, pred[48]{0:T(512)(128)(4,1)S(1)}, u32[]{:S(2)}) copy-start(pred[48]{0:T(512)(128)(4,1)S(1)} %compare_and_fusion) | copy-start | bytes 148
  92.6 4.7 %copy-start.8 = (s32[1,1,48]{2,1,0:T(1,128)S(1)}, s32[1,1,48]{2,1,0:T(1,128)}, u32[]{:S(2)}) copy-start(s32[1,1,48]{2,1,0:T(1,128)} %param.16) | copy-start | bytes 580
  98.9 37.8 %copy-start.1 = (f32[32,4096]{1,0:T(8,128)S(1)}, f32[32,4096]{1,0:T(8,128)}, u32[]{:S(2)}) copy-start(f32[32,4096]{1,0:T(8,128)} %param.20) | copy-start | bytes 1572868
  98.9 37.8 %copy-start.15 = (f32[32]{0:T(128)S(1)}, f32[32]{0:T(128)}, u32[]{:S(2)}) copy-start(f32[32]{0:T(128)} %param.25) | copy-start | bytes 388
  99.8 113.8 %all-reduce.6.cloned.1.call-start = ((), (), s32[]{:S(2)}) async-start(), calls=%async_computation.2 | async-start | bytes 4194304 | tf_op jit(solution)/shard_map/psum | solution.py:34
  139.6 4.3 %copy-start.22 = (s32[1,1,48]{2,1,0:T(1,128)S(1)}, s32[1,1,48]{2,1,0:T(1,128)}, u32[]{:S(2)}) copy-start(s32[1,1,48]{2,1,0:T(1,128)} %param.17) | copy-start | bytes 580
  148.6 65.0 %copy-start.19 = (f32[32]{0:T(128)S(1)}, f32[32]{0:T(128)}, u32[]{:S(2)}) copy-start(f32[32]{0:T(128)} %param.24) | copy-start | bytes 388
  148.6 116.5 %all-gather.6.cloned.1.call-start = ((), (), s32[]{:S(2)}) async-start(), calls=%async_computation.3 | async-start | bytes 2621440 | tf_op jit(solution)/shard_map/all_gather | solution.py:48
  216.7 4.0 copy-start.12
  220.7 5.0 %copy-start.9 = (s32[1,1,48]{2,1,0:T(1,128)S(1)}, s32[1,1,48]{2,1,0:T(1,128)}, u32[]{:S(2)}) copy-start(s32[1,1,48]{2,1,0:T(1,128)} %param.16) | copy-start | bytes 580
  228.1 39.6 %copy-start.16 = (f32[32]{0:T(128)S(1)}, f32[32]{0:T(128)}, u32[]{:S(2)}) copy-start(f32[32]{0:T(128)} %param.25) | copy-start | bytes 388
  230.0 114.9 %all-reduce.8.cloned.1.call-start = ((), (), s32[]{:S(2)}) async-start(), calls=%async_computation.4 | async-start | bytes 4194304 | tf_op jit(solution)/shard_map/psum | solution.py:34
  270.8 4.3 %copy-start.23 = (s32[1,1,48]{2,1,0:T(1,128)S(1)}, s32[1,1,48]{2,1,0:T(1,128)}, u32[]{:S(2)}) copy-start(s32[1,1,48]{2,1,0:T(1,128)} %param.17) | copy-start | bytes 580
  279.8 65.1 %copy-start.20 = (f32[32]{0:T(128)S(1)}, f32[32]{0:T(128)}, u32[]{:S(2)}) copy-start(f32[32]{0:T(128)} %param.24) | copy-start | bytes 388
  279.8 114.9 %all-gather.8.cloned.1.call-start = ((), (), s32[]{:S(2)}) async-start(), calls=%async_computation.5 | async-start | bytes 2621440 | tf_op jit(solution)/shard_map/all_gather | solution.py:48
  350.3 1.8 copy-start.13
  352.1 5.0 %copy-start.10 = (s32[1,1,48]{2,1,0:T(1,128)S(1)}, s32[1,1,48]{2,1,0:T(1,128)}, u32[]{:S(2)}) copy-start(s32[1,1,48]{2,1,0:T(1,128)} %param.16) | copy-start | bytes 580
  358.7 37.8 %copy-start.2 = (f32[32,4096]{1,0:T(8,128)S(1)}, f32[32,4096]{1,0:T(8,128)}, u32[]{:S(2)}) copy-start(f32[32,4096]{1,0:T(8,128)} %param.23) | copy-start | bytes 1572868
  358.7 37.8 %copy-start.3 = (f32[32,4096]{1,0:T(8,128)S(1)}, f32[32,4096]{1,0:T(8,128)}, u32[]{:S(2)}) copy-start(f32[32,4096]{1,0:T(8,128)} %reduce_sum.28) | copy-start | bytes 1572868
  358.7 37.8 %copy-start.17 = (f32[32]{0:T(128)S(1)}, f32[32]{0:T(128)}, u32[]{:S(2)}) copy-start(f32[32]{0:T(128)} %param.25) | copy-start | bytes 388
Sparse Core Ops, SparseCore 0:
  19.8 67.5 all-reduce.3
  99.9 34.9 all-gather.3
  148.7 64.8 all-reduce.5
  230.1 34.9 all-gather.5
  279.9 64.9 all-reduce.7
  359.7 34.9 all-gather.7
